TPU v7x, 128 devices: a whole 4x4x4 slice. The times are simulated.
128 devices in a mesh: section: 8 (over y, core), edge: 16 (over z, x).
Axes of the slice: x: 4, y: 4, z: 4, core: 2. Of those that a mesh axis runs over, the one named last changes fastest.
Arguments:
- layer_nodes: bfloat16 [8, 2, 256, 512], P('section'), may hold values from -6 to 6
- layer_edges: bfloat16 [8, 2, 4096, 512], P('section', None, 'edge'), may hold values from -6 to 6
- top_nodes: bfloat16 [2, 256, 512], replicated, may hold values from -1.5 to 1.5
- top_edges: bfloat16 [2, 4096, 512], P(None, 'edge'), may hold values from -1.5 to 1.5
- tile_blocks: int32 [2, 32, 2], P(None, 'edge'), may hold values from 0 to 1
- senders: int32 [2, 4096], P(None, 'edge'), may hold values from 0 to 127
- receivers: int32 [2, 4096], P(None, 'edge'), may hold values from 0 to 127
- w_send: bfloat16 [8, 512, 512], P('section'), may hold values from -0.0625 to 0.0625
- w_recv: bfloat16 [8, 512, 512], P('section'), may hold values from -0.0625 to 0.0625
- w_edge: bfloat16 [8, 512, 512], P('section'), may hold values from -0.25 to 0.25
- w_msg: bfloat16 [8, 512, 512], P('section'), may hold values from -0.125 to 0.125
- w_node: bfloat16 [8, 512, 512], P('section'), may hold values from -0.25 to 0.25
- w_agg: bfloat16 [8, 512, 512], P('section'), may hold values from -0.25 to 0.25
- w_out: bfloat16 [8, 512, 512], P('section'), may hold values from -0.125 to 0.125
Outputs:
- node_grads: bfloat16 [8, 2, 256, 512], P('section', None, 'edge')
- edge_grads: bfloat16 [8, 2, 4096, 512], P('section', None, 'edge')
- g_send: float32 [8, 512, 512], P('section', 'edge')
- g_recv: float32 [8, 512, 512], P('section', 'edge')
- g_edge: float32 [8, 512, 512], P('section', 'edge')
- g_msg: float32 [8, 512, 512], P('section', 'edge')
- g_node: float32 [8, 512, 512], P('section', 'edge')
- g_agg: float32 [8, 512, 512], P('section', 'edge')
- g_out: float32 [8, 512, 512], P('section', 'edge')
All inputs are finite; a program needn't handle non-finite values.
Results may differ from a plain program's by a relative error of at most 0.029.
Values may be sent and summed in bfloat16 or wider, within the bound.
A program may use at most 64 MiB of HBM per device.

v0:
```python
import jax
import jax.numpy as jnp
from jax import lax
from jax.sharding import PartitionSpec as P

BLOCK = 128


def shifted(shard, axis, by):
    peers = lax.axis_size(axis)
    pairs = [(i, i + by) for i in range(peers) if 0 <= i + by < peers]
    return lax.ppermute(shard, axis, pairs)


def silu_slope(values):
    sigma = jax.nn.sigmoid(values)
    return sigma * (1.0 + values * (1.0 - sigma))


def matmul(left, right):
    return jnp.dot(left, right, preferred_element_type=jnp.float32)


def times_transposed(left, right):
    return lax.dot_general(
        left, right, (((1,), (1,)), ((), ())), preferred_element_type=jnp.float32
    )


def transposed_times(left, right):
    return lax.dot_general(
        left, right, (((0,), (0,)), ((), ())), preferred_element_type=jnp.float32
    )


def to_edges(values, block_hot, edge_hot):
    width = values.shape[1]
    grouped = values.reshape(block_hot.shape[1], -1, width)
    picked = jnp.einsum(
        "tb,bcd->tcd", block_hot, grouped, preferred_element_type=jnp.float32
    ).astype(jnp.bfloat16)
    spread = jnp.einsum("tec,tcd->ted", edge_hot, picked, preferred_element_type=jnp.float32)
    return spread.reshape(-1, width).astype(jnp.bfloat16)


def to_nodes(values, block_hot, edge_hot):
    width = values.shape[1]
    per_tile = jnp.einsum(
        "tec,ted->tcd",
        edge_hot,
        values.reshape(block_hot.shape[0], -1, width),
        preferred_element_type=jnp.float32,
    )
    summed = jnp.einsum(
        "tb,tcd->bcd", block_hot.astype(jnp.float32), per_tile, precision=lax.Precision.HIGHEST
    )
    return summed.reshape(-1, width)


def body(
    layer_nodes,
    layer_edges,
    top_nodes,
    top_edges,
    tile_blocks,
    senders,
    receivers,
    w_send,
    w_recv,
    w_edge,
    w_msg,
    w_node,
    w_agg,
    w_out,
):
    sections = lax.axis_size("section")
    section = lax.axis_index("section")
    groups = lax.axis_size("edge")
    member = lax.axis_index("edge")
    nodes_all = layer_nodes[0]
    edges_all = layer_edges[0]
    batches = nodes_all.shape[0]
    node_count = nodes_all.shape[1]
    width = nodes_all.shape[2]
    tile_count = tile_blocks.shape[1]
    tile_len = edges_all.shape[1] // tile_count
    block_count = node_count // BLOCK
    row_count = node_count // groups
    weight_send, weight_recv, weight_edge, weight_msg = (w_send[0], w_recv[0], w_edge[0], w_msg[0])
    weight_node, weight_agg, weight_out = (w_node[0], w_agg[0], w_out[0])
    lanes = jnp.arange(BLOCK, dtype=jnp.int32)
    slots = jnp.arange(block_count, dtype=jnp.int32)
    send_hot = (senders.reshape(batches, tile_count, tile_len)[..., None] == lanes).astype(
        jnp.bfloat16
    )
    recv_hot = (receivers.reshape(batches, tile_count, tile_len)[..., None] == lanes).astype(
        jnp.bfloat16
    )
    send_block = (tile_blocks[:, :, 0][..., None] == slots).astype(jnp.bfloat16)
    recv_block = (tile_blocks[:, :, 1][..., None] == slots).astype(jnp.bfloat16)

    def advance(moment, carry):
        node_in_grad, edge_in_grad, totals, node_record, edge_record = carry
        batch_raw = moment - (sections - 1 - section)
        valid = (batch_raw >= 0) & (batch_raw < batches)
        batch = jnp.clip(batch_raw, 0, batches - 1)
        feats = lax.dynamic_index_in_dim(nodes_all, batch, 0, keepdims=False)
        edge_feats = lax.dynamic_index_in_dim(edges_all, batch, 0, keepdims=False)
        send_tiles = lax.dynamic_index_in_dim(send_hot, batch, 0, keepdims=False)
        recv_tiles = lax.dynamic_index_in_dim(recv_hot, batch, 0, keepdims=False)
        send_blocks = lax.dynamic_index_in_dim(send_block, batch, 0, keepdims=False)
        recv_blocks = lax.dynamic_index_in_dim(recv_block, batch, 0, keepdims=False)
        top_node = lax.dynamic_index_in_dim(top_nodes, batch, 0, keepdims=False)
        top_edge = lax.dynamic_index_in_dim(top_edges, batch, 0, keepdims=False)
        is_last = section == sections - 1
        grad_nodes = jnp.where(is_last, top_node, node_in_grad)
        grad_edges = jnp.where(is_last, top_edge, edge_in_grad)
        send_feats = to_edges(feats, send_blocks, send_tiles)
        recv_feats = to_edges(feats, recv_blocks, recv_tiles)
        pre = (
            matmul(send_feats, weight_send)
            + matmul(recv_feats, weight_recv)
            + matmul(edge_feats, weight_edge)
        )
        act = jax.nn.silu(pre).astype(jnp.bfloat16)
        message = matmul(act, weight_msg).astype(jnp.bfloat16)
        partial_agg = to_nodes(message, recv_blocks, recv_tiles)
        aggregate = lax.psum(partial_agg, "edge")
        agg_b = aggregate.astype(jnp.bfloat16)
        node_pre = matmul(feats, weight_node) + matmul(agg_b, weight_agg)
        node_act = jax.nn.silu(node_pre).astype(jnp.bfloat16)
        node_delta = (times_transposed(grad_nodes, weight_out) * silu_slope(node_pre)).astype(
            jnp.bfloat16
        )
        agg_grad = times_transposed(node_delta, weight_agg).astype(jnp.bfloat16)
        node_term = times_transposed(node_delta, weight_node)
        agg_edges = to_edges(agg_grad, recv_blocks, recv_tiles)
        message_grad = (grad_edges.astype(jnp.float32) + agg_edges.astype(jnp.float32)).astype(
            jnp.bfloat16
        )
        edge_delta = (times_transposed(message_grad, weight_msg) * silu_slope(pre)).astype(
            jnp.bfloat16
        )
        edge_out = (
            grad_edges.astype(jnp.float32) + times_transposed(edge_delta, weight_edge)
        ).astype(jnp.bfloat16)
        send_grad = times_transposed(edge_delta, weight_send).astype(jnp.bfloat16)
        recv_grad = times_transposed(edge_delta, weight_recv).astype(jnp.bfloat16)
        partial_back = to_nodes(send_grad, send_blocks, send_tiles) + to_nodes(
            recv_grad, recv_blocks, recv_tiles
        )
        edge_terms = lax.psum(partial_back, "edge")
        node_out = (grad_nodes.astype(jnp.float32) + node_term + edge_terms).astype(jnp.bfloat16)
        fresh = (
            transposed_times(send_feats, edge_delta),
            transposed_times(recv_feats, edge_delta),
            transposed_times(edge_feats, edge_delta),
            transposed_times(act, message_grad),
            transposed_times(feats, node_delta),
            transposed_times(agg_b, node_delta),
            transposed_times(node_act, grad_nodes),
        )
        totals = tuple(
            (jnp.where(valid, before + extra, before) for before, extra in zip(totals, fresh))
        )
        own_out = lax.dynamic_slice_in_dim(node_out, member * row_count, row_count, 0)
        node_record = jnp.where(
            valid, lax.dynamic_update_index_in_dim(node_record, own_out, batch, 0), node_record
        )
        edge_record = jnp.where(
            valid, lax.dynamic_update_index_in_dim(edge_record, edge_out, batch, 0), edge_record
        )
        sent_nodes, sent_edges = shifted((node_out, edge_out), "section", -1)
        return (sent_nodes, sent_edges, totals, node_record, edge_record)

    hidden = weight_send.shape[1]
    square_in = jnp.zeros((width, hidden), jnp.float32)
    square_back = jnp.zeros((hidden, width), jnp.float32)
    start = (
        jnp.zeros((node_count, width), jnp.bfloat16),
        jnp.zeros(edges_all.shape[1:], jnp.bfloat16),
        (square_in, square_in, square_in, square_back, square_in, square_in, square_back),
        jnp.zeros((batches, row_count, width), jnp.bfloat16),
        jnp.zeros(edges_all.shape, jnp.bfloat16),
    )
    finished = lax.fori_loop(0, sections + batches - 1, advance, start)
    totals, node_record, edge_record = (finished[2], finished[3], finished[4])
    sum_send, sum_recv, sum_edge, sum_msg, sum_node, sum_agg, sum_out = totals
    sum_send, sum_recv, sum_edge, sum_msg = (
        lax.psum_scatter(sum_send, "edge", scatter_dimension=0, tiled=True),
        lax.psum_scatter(sum_recv, "edge", scatter_dimension=0, tiled=True),
        lax.psum_scatter(sum_edge, "edge", scatter_dimension=0, tiled=True),
        lax.psum_scatter(sum_msg, "edge", scatter_dimension=0, tiled=True),
    )
    sum_node = lax.dynamic_slice_in_dim(sum_node, member * (width // groups), width // groups, 0)
    sum_agg = lax.dynamic_slice_in_dim(sum_agg, member * (width // groups), width // groups, 0)
    sum_out = lax.dynamic_slice_in_dim(sum_out, member * (hidden // groups), hidden // groups, 0)
    return (
        node_record[None],
        edge_record[None],
        sum_send[None],
        sum_recv[None],
        sum_edge[None],
        sum_msg[None],
        sum_node[None],
        sum_agg[None],
        sum_out[None],
    )


def solution(mesh):
    in_specs = (
        P("section", None, None, None),
        P("section", None, "edge", None),
        P(),
        P(None, "edge", None),
        P(None, "edge", None),
        P(None, "edge"),
        P(None, "edge"),
        P("section", None, None),
        P("section", None, None),
        P("section", None, None),
        P("section", None, None),
        P("section", None, None),
        P("section", None, None),
        P("section", None, None),
    )
    out_specs = (
        P("section", None, "edge", None),
        P("section", None, "edge", None),
        P("section", "edge", None),
        P("section", "edge", None),
        P("section", "edge", None),
        P("section", "edge", None),
        P("section", "edge", None),
        P("section", "edge", None),
        P("section", "edge", None),
    )
    return jax.shard_map(body, mesh=mesh, in_specs=in_specs, out_specs=out_specs, check_vma=False)
```

profile of v0, /device:TPU:0, one launch (start us, length us, event | category | flops | bytes accessed | tf_op | source)
XLA Modules:
  0.0 2031.3 jit_solution(16253940211328947030)
XLA Ops:
  13.3 1701.8 %while.36 = (s32[]{:T(128)}, bf16[256,512]{1,0:T(8,128)(2,1)S(1)}, bf16[256,512]{1,0:T(8,128)(2,1)S(1)}, f32[512,512]{1,0:T(8,128)}, f32[512,512]{1,0:T(8,128)},...) while((s32[]{:T(128)}, bf16[256,512]{1,0:T(8,128)(2,1)S(1)}, ...), condition=%wide.region_3.4_spmd.clone, body=%wide.region_0.3_spmd.clone.sunk | while | flops 2910199808 | bytes 137546704 | solution.py:186
  21.1 81.4 %all-reduce.4 = bf16[256,512]{1,0:T(8,128)(2,1)S(1)} all-reduce(f32[256,512]{1,0:T(8,128)S(1)} %bitcast.271), channel_id=1, replica_groups=mesh['section'=8,'edge'=16] {'edge'}, use_global_device_ids=true, to_apply=%region_1.1 | all-reduce | flops 131072 | bytes 786432 | tf_op jit(solution)/shard_map/while/body/eval_jaxpr/psum | solution.py:128
  129.5 69.2 %all-reduce.3.cloned.1.call-done = f32[256,512]{1,0:T(8,128)} async-done(((f32[256,512]{1,0:T(8,128)}), f32[256,512]{1,0:T(8,128)}) %all-reduce.3.cloned.1.call-update) | async-done | bytes 524304 | tf_op jit(solution)/shard_map/while/body/eval_jaxpr/psum | solution.py:152
  211.4 77.6 %all-reduce.4 = bf16[256,512]{1,0:T(8,128)(2,1)S(1)} all-reduce(f32[256,512]{1,0:T(8,128)S(1)} %bitcast.271), channel_id=1, replica_groups=mesh['section'=8,'edge'=16] {'edge'}, use_global_device_ids=true, to_apply=%region_1.1 | all-reduce | flops 131072 | bytes 786432 | tf_op jit(solution)/shard_map/while/body/eval_jaxpr/psum | solution.py:128
  317.5 70.1 %all-reduce.3.cloned.1.call-done = f32[256,512]{1,0:T(8,128)} async-done(((f32[256,512]{1,0:T(8,128)}), f32[256,512]{1,0:T(8,128)}) %all-reduce.3.cloned.1.call-update) | async-done | bytes 524304 | tf_op jit(solution)/shard_map/while/body/eval_jaxpr/psum | solution.py:152
  400.3 77.6 %all-reduce.4 = bf16[256,512]{1,0:T(8,128)(2,1)S(1)} all-reduce(f32[256,512]{1,0:T(8,128)S(1)} %bitcast.271), channel_id=1, replica_groups=mesh['section'=8,'edge'=16] {'edge'}, use_global_device_ids=true, to_apply=%region_1.1 | all-reduce | flops 131072 | bytes 786432 | tf_op jit(solution)/shard_map/while/body/eval_jaxpr/psum | solution.py:128
  506.5 70.1 %all-reduce.3.cloned.1.call-done = f32[256,512]{1,0:T(8,128)} async-done(((f32[256,512]{1,0:T(8,128)}), f32[256,512]{1,0:T(8,128)}) %all-reduce.3.cloned.1.call-update) | async-done | bytes 524304 | tf_op jit(solution)/shard_map/while/body/eval_jaxpr/psum | solution.py:152
  589.3 77.6 %all-reduce.4 = bf16[256,512]{1,0:T(8,128)(2,1)S(1)} all-reduce(f32[256,512]{1,0:T(8,128)S(1)} %bitcast.271), channel_id=1, replica_groups=mesh['section'=8,'edge'=16] {'edge'}, use_global_device_ids=true, to_apply=%region_1.1 | all-reduce | flops 131072 | bytes 786432 | tf_op jit(solution)/shard_map/while/body/eval_jaxpr/psum | solution.py:128
  695.4 70.1 %all-reduce.3.cloned.1.call-done = f32[256,512]{1,0:T(8,128)} async-done(((f32[256,512]{1,0:T(8,128)}), f32[256,512]{1,0:T(8,128)}) %all-reduce.3.cloned.1.call-update) | async-done | bytes 524304 | tf_op jit(solution)/shard_map/while/body/eval_jaxpr/psum | solution.py:152
  778.2 77.6 %all-reduce.4 = bf16[256,512]{1,0:T(8,128)(2,1)S(1)} all-reduce(f32[256,512]{1,0:T(8,128)S(1)} %bitcast.271), channel_id=1, replica_groups=mesh['section'=8,'edge'=16] {'edge'}, use_global_device_ids=true, to_apply=%region_1.1 | all-reduce | flops 131072 | bytes 786432 | tf_op jit(solution)/shard_map/while/body/eval_jaxpr/psum | solution.py:128
  884.4 70.1 %all-reduce.3.cloned.1.call-done = f32[256,512]{1,0:T(8,128)} async-done(((f32[256,512]{1,0:T(8,128)}), f32[256,512]{1,0:T(8,128)}) %all-reduce.3.cloned.1.call-update) | async-done | bytes 524304 | tf_op jit(solution)/shard_map/while/body/eval_jaxpr/psum | solution.py:152
  967.2 77.6 %all-reduce.4 = bf16[256,512]{1,0:T(8,128)(2,1)S(1)} all-reduce(f32[256,512]{1,0:T(8,128)S(1)} %bitcast.271), channel_id=1, replica_groups=mesh['section'=8,'edge'=16] {'edge'}, use_global_device_ids=true, to_apply=%region_1.1 | all-reduce | flops 131072 | bytes 786432 | tf_op jit(solution)/shard_map/while/body/eval_jaxpr/psum | solution.py:128
  1073.3 70.1 %all-reduce.3.cloned.1.call-done = f32[256,512]{1,0:T(8,128)} async-done(((f32[256,512]{1,0:T(8,128)}), f32[256,512]{1,0:T(8,128)}) %all-reduce.3.cloned.1.call-update) | async-done | bytes 524304 | tf_op jit(solution)/shard_map/while/body/eval_jaxpr/psum | solution.py:152
  1156.1 77.6 %all-reduce.4 = bf16[256,512]{1,0:T(8,128)(2,1)S(1)} all-reduce(f32[256,512]{1,0:T(8,128)S(1)} %bitcast.271), channel_id=1, replica_groups=mesh['section'=8,'edge'=16] {'edge'}, use_global_device_ids=true, to_apply=%region_1.1 | all-reduce | flops 131072 | bytes 786432 | tf_op jit(solution)/shard_map/while/body/eval_jaxpr/psum | solution.py:128
  1262.3 70.1 %all-reduce.3.cloned.1.call-done = f32[256,512]{1,0:T(8,128)} async-done(((f32[256,512]{1,0:T(8,128)}), f32[256,512]{1,0:T(8,128)}) %all-reduce.3.cloned.1.call-update) | async-done | bytes 524304 | tf_op jit(solution)/shard_map/while/body/eval_jaxpr/psum | solution.py:152
  1345.1 77.6 %all-reduce.4 = bf16[256,512]{1,0:T(8,128)(2,1)S(1)} all-reduce(f32[256,512]{1,0:T(8,128)S(1)} %bitcast.271), channel_id=1, replica_groups=mesh['section'=8,'edge'=16] {'edge'}, use_global_device_ids=true, to_apply=%region_1.1 | all-reduce | flops 131072 | bytes 786432 | tf_op jit(solution)/shard_map/while/body/eval_jaxpr/psum | solution.py:128
  1440.4 2.9 add_select_fusion.17
  1451.2 70.1 %all-reduce.3.cloned.1.call-done = f32[256,512]{1,0:T(8,128)} async-done(((f32[256,512]{1,0:T(8,128)}), f32[256,512]{1,0:T(8,128)}) %all-reduce.3.cloned.1.call-update) | async-done | bytes 524304 | tf_op jit(solution)/shard_map/while/body/eval_jaxpr/psum | solution.py:152
  1534.1 77.6 %all-reduce.4 = bf16[256,512]{1,0:T(8,128)(2,1)S(1)} all-reduce(f32[256,512]{1,0:T(8,128)S(1)} %bitcast.271), channel_id=1, replica_groups=mesh['section'=8,'edge'=16] {'edge'}, use_global_device_ids=true, to_apply=%region_1.1 | all-reduce | flops 131072 | bytes 786432 | tf_op jit(solution)/shard_map/while/body/eval_jaxpr/psum | solution.py:128
  1640.2 70.1 %all-reduce.3.cloned.1.call-done = f32[256,512]{1,0:T(8,128)} async-done(((f32[256,512]{1,0:T(8,128)}), f32[256,512]{1,0:T(8,128)}) %all-reduce.3.cloned.1.call-update) | async-done | bytes 524304 | tf_op jit(solution)/shard_map/while/body/eval_jaxpr/psum | solution.py:152
  1722.0 73.1 %reduce-scatter.5.cloned.1.call-done = f32[32,512]{1,0:T(8,128)} async-done(((f32[512,512]{1,0:T(8,128)}), f32[32,512]{1,0:T(8,128)}) %reduce-scatter.5.cloned.1.call-update) | async-done | bytes 65552 | tf_op jit(solution)/shard_map/reduce_scatter | solution.py:190
  1795.1 76.3 %reduce-scatter.7.cloned.1.call-done = f32[32,512]{1,0:T(8,128)} async-done(((f32[512,512]{1,0:T(8,128)}), f32[32,512]{1,0:T(8,128)}) %reduce-scatter.7.cloned.1.call-update) | async-done | bytes 65552 | tf_op jit(solution)/shard_map/reduce_scatter | solution.py:191
  1871.4 76.0 %reduce-scatter.9.cloned.1.call-done = f32[32,512]{1,0:T(8,128)} async-done(((f32[512,512]{1,0:T(8,128)}), f32[32,512]{1,0:T(8,128)}) %reduce-scatter.9.cloned.1.call-update) | async-done | bytes 65552 | tf_op jit(solution)/shard_map/reduce_scatter | solution.py:192
  1947.4 76.5 %reduce-scatter.11.cloned.1.call-done = f32[32,512]{1,0:T(8,128)} async-done(((f32[512,512]{1,0:T(8,128)}), f32[32,512]{1,0:T(8,128)}) %reduce-scatter.11.cloned.1.call-update) | async-done | bytes 65552 | tf_op jit(solution)/shard_map/reduce_scatter | solution.py:193
  (999 shorter events, 374.4 us)
Async XLA Ops:
  13.3 185.4 %all-reduce.3.cloned.1.call-start = ((), (), s32[]{:S(2)}) async-start(), calls=%async_computation.8 | async-start | bytes 1048576 | tf_op jit(solution)/shard_map/while/body/eval_jaxpr/psum | solution.py:152
  119.0 83.2 %collective-permute-start.1 = (bf16[256,512]{1,0:T(8,128)(2,1)}, bf16[256,512]{1,0:T(8,128)(2,1)S(1)}, u32[]{:S(2)}, u32[]{:S(2)}) collective-permute-start(bf16[256,512]{1,0:T(8,128)(2,1)} %get-tuple-element.1012), channel_id=1, source_target_pairs={{16,0},{32,16},{48,32},{64,48},{80,64},{96,80},{112,96},{17,1},{33... | collective-permute-start | bytes 786440 | tf_op jit(solution)/shard_map/while/body/eval_jaxpr/ppermute | solution.py:12
  203.5 184.1 %all-reduce.3.cloned.1.call-start = ((), (), s32[]{:S(2)}) async-start(), calls=%async_computation.8 | async-start | bytes 1048576 | tf_op jit(solution)/shard_map/while/body/eval_jaxpr/psum | solution.py:152
  305.4 85.7 %collective-permute-start.1 = (bf16[256,512]{1,0:T(8,128)(2,1)}, bf16[256,512]{1,0:T(8,128)(2,1)S(1)}, u32[]{:S(2)}, u32[]{:S(2)}) collective-permute-start(bf16[256,512]{1,0:T(8,128)(2,1)} %get-tuple-element.1012), channel_id=1, source_target_pairs={{16,0},{32,16},{48,32},{64,48},{80,64},{96,80},{112,96},{17,1},{33... | collective-permute-start | bytes 786440 | tf_op jit(solution)/shard_map/while/body/eval_jaxpr/ppermute | solution.py:12
  392.5 184.1 %all-reduce.3.cloned.1.call-start = ((), (), s32[]{:S(2)}) async-start(), calls=%async_computation.8 | async-start | bytes 1048576 | tf_op jit(solution)/shard_map/while/body/eval_jaxpr/psum | solution.py:152
  494.4 85.7 %collective-permute-start.1 = (bf16[256,512]{1,0:T(8,128)(2,1)}, bf16[256,512]{1,0:T(8,128)(2,1)S(1)}, u32[]{:S(2)}, u32[]{:S(2)}) collective-permute-start(bf16[256,512]{1,0:T(8,128)(2,1)} %get-tuple-element.1012), channel_id=1, source_target_pairs={{16,0},{32,16},{48,32},{64,48},{80,64},{96,80},{112,96},{17,1},{33... | collective-permute-start | bytes 786440 | tf_op jit(solution)/shard_map/while/body/eval_jaxpr/ppermute | solution.py:12
  578.0 3.4 collective-permute-start
  581.4 184.1 %all-reduce.3.cloned.1.call-start = ((), (), s32[]{:S(2)}) async-start(), calls=%async_computation.8 | async-start | bytes 1048576 | tf_op jit(solution)/shard_map/while/body/eval_jaxpr/psum | solution.py:152
  683.3 85.7 %collective-permute-start.1 = (bf16[256,512]{1,0:T(8,128)(2,1)}, bf16[256,512]{1,0:T(8,128)(2,1)S(1)}, u32[]{:S(2)}, u32[]{:S(2)}) collective-permute-start(bf16[256,512]{1,0:T(8,128)(2,1)} %get-tuple-element.1012), channel_id=1, source_target_pairs={{16,0},{32,16},{48,32},{64,48},{80,64},{96,80},{112,96},{17,1},{33... | collective-permute-start | bytes 786440 | tf_op jit(solution)/shard_map/while/body/eval_jaxpr/ppermute | solution.py:12
  766.9 3.4 collective-permute-start
  770.4 184.1 %all-reduce.3.cloned.1.call-start = ((), (), s32[]{:S(2)}) async-start(), calls=%async_computation.8 | async-start | bytes 1048576 | tf_op jit(solution)/shard_map/while/body/eval_jaxpr/psum | solution.py:152
  872.3 85.7 %collective-permute-start.1 = (bf16[256,512]{1,0:T(8,128)(2,1)}, bf16[256,512]{1,0:T(8,128)(2,1)S(1)}, u32[]{:S(2)}, u32[]{:S(2)}) collective-permute-start(bf16[256,512]{1,0:T(8,128)(2,1)} %get-tuple-element.1012), channel_id=1, source_target_pairs={{16,0},{32,16},{48,32},{64,48},{80,64},{96,80},{112,96},{17,1},{33... | collective-permute-start | bytes 786440 | tf_op jit(solution)/shard_map/while/body/eval_jaxpr/ppermute | solution.py:12
  959.3 184.1 %all-reduce.3.cloned.1.call-start = ((), (), s32[]{:S(2)}) async-start(), calls=%async_computation.8 | async-start | bytes 1048576 | tf_op jit(solution)/shard_map/while/body/eval_jaxpr/psum | solution.py:152
  1061.2 85.7 %collective-permute-start.1 = (bf16[256,512]{1,0:T(8,128)(2,1)}, bf16[256,512]{1,0:T(8,128)(2,1)S(1)}, u32[]{:S(2)}, u32[]{:S(2)}) collective-permute-start(bf16[256,512]{1,0:T(8,128)(2,1)} %get-tuple-element.1012), channel_id=1, source_target_pairs={{16,0},{32,16},{48,32},{64,48},{80,64},{96,80},{112,96},{17,1},{33... | collective-permute-start | bytes 786440 | tf_op jit(solution)/shard_map/while/body/eval_jaxpr/ppermute | solution.py:12
  1148.3 184.1 %all-reduce.3.cloned.1.call-start = ((), (), s32[]{:S(2)}) async-start(), calls=%async_computation.8 | async-start | bytes 1048576 | tf_op jit(solution)/shard_map/while/body/eval_jaxpr/psum | solution.py:152
  1250.2 85.7 %collective-permute-start.1 = (bf16[256,512]{1,0:T(8,128)(2,1)}, bf16[256,512]{1,0:T(8,128)(2,1)S(1)}, u32[]{:S(2)}, u32[]{:S(2)}) collective-permute-start(bf16[256,512]{1,0:T(8,128)(2,1)} %get-tuple-element.1012), channel_id=1, source_target_pairs={{16,0},{32,16},{48,32},{64,48},{80,64},{96,80},{112,96},{17,1},{33... | collective-permute-start | bytes 786440 | tf_op jit(solution)/shard_map/while/body/eval_jaxpr/ppermute | solution.py:12
  1337.2 184.1 %all-reduce.3.cloned.1.call-start = ((), (), s32[]{:S(2)}) async-start(), calls=%async_computation.8 | async-start | bytes 1048576 | tf_op jit(solution)/shard_map/while/body/eval_jaxpr/psum | solution.py:152
  1439.1 85.7 %collective-permute-start.1 = (bf16[256,512]{1,0:T(8,128)(2,1)}, bf16[256,512]{1,0:T(8,128)(2,1)S(1)}, u32[]{:S(2)}, u32[]{:S(2)}) collective-permute-start(bf16[256,512]{1,0:T(8,128)(2,1)} %get-tuple-element.1012), channel_id=1, source_target_pairs={{16,0},{32,16},{48,32},{64,48},{80,64},{96,80},{112,96},{17,1},{33... | collective-permute-start | bytes 786440 | tf_op jit(solution)/shard_map/while/body/eval_jaxpr/ppermute | solution.py:12
  1526.2 184.1 %all-reduce.3.cloned.1.call-start = ((), (), s32[]{:S(2)}) async-start(), calls=%async_computation.8 | async-start | bytes 1048576 | tf_op jit(solution)/shard_map/while/body/eval_jaxpr/psum | solution.py:152
  1628.1 85.7 %collective-permute-start.1 = (bf16[256,512]{1,0:T(8,128)(2,1)}, bf16[256,512]{1,0:T(8,128)(2,1)S(1)}, u32[]{:S(2)}, u32[]{:S(2)}) collective-permute-start(bf16[256,512]{1,0:T(8,128)(2,1)} %get-tuple-element.1012), channel_id=1, source_target_pairs={{16,0},{32,16},{48,32},{64,48},{80,64},{96,80},{112,96},{17,1},{33... | collective-permute-start | bytes 786440 | tf_op jit(solution)/shard_map/while/body/eval_jaxpr/ppermute | solution.py:12
  1715.1 80.0 %reduce-scatter.5.cloned.1.call-start = ((), (), s32[]{:S(2)}) async-start(), calls=%async_computation.4 | async-start | bytes 1114112 | tf_op jit(solution)/shard_map/reduce_scatter | solution.py:190
  1715.7 155.7 %reduce-scatter.7.cloned.1.call-start = ((), (), s32[]{:S(2)}) async-start(), calls=%async_computation.5 | async-start | bytes 1114112 | tf_op jit(solution)/shard_map/reduce_scatter | solution.py:191
  1716.3 231.1 %reduce-scatter.9.cloned.1.call-start = ((), (), s32[]{:S(2)}) async-start(), calls=%async_computation.6 | async-start | bytes 1114112 | tf_op jit(solution)/shard_map/reduce_scatter | solution.py:192
  1716.9 307.1 %reduce-scatter.11.cloned.1.call-start = ((), (), s32[]{:S(2)}) async-start(), calls=%async_computation.7 | async-start | bytes 1114112 | tf_op jit(solution)/shard_map/reduce_scatter | solution.py:193
  (291 other events, 1022.0 us)
Sparse Core Ops, SparseCore 0:
  115.9 82.6 all-reduce.2
  302.4 85.1 all-reduce.2
  491.3 85.1 all-reduce.2
  680.3 85.1 all-reduce.2
  869.2 85.1 all-reduce.2
  1058.2 85.1 all-reduce.2
  1247.1 85.1 all-reduce.2
  1436.1 85.1 all-reduce.2
  1625.0 85.1 all-reduce.2
Sparse Core Ops, SparseCore 1:
  1719.4 75.7 reduce-scatter.4
  1799.1 72.2 reduce-scatter.6
  1875.0 72.3 reduce-scatter.8
  1951.5 72.4 reduce-scatter.10
where the time goes:
time: 2040 us; the launch traced here: 2030 us
  waiting for transfers between devices  946 us (46%)
  blocking collectives  702 us (34%)
  matrix products  214 us (10%)
  local copies, waits for them, and re-layouts  123 us (6%)
  starting transfers between devices  23.3 us (1%)
    psum x9, blocking collectives, advance(): aggregate = lax.psum(partial_agg, 'edge')  702 us
    psum x9, waiting for transfers between devices, advance(): edge_terms = lax.psum(partial_back, 'edge')  630 us
    while x558, local copies, waits for them, and re-layouts  96.3 us
    reduce_scatter x1, waiting for transfers between devices, body(): lax.psum_scatter(sum_msg, 'edge', scatter_dimension=0, tiled=True)  76.5 us
    reduce_scatter x1, waiting for transfers between devices, body(): lax.psum_scatter(sum_recv, 'edge', scatter_dimension=0, tiled=True)  76.3 us
    reduce_scatter x1, waiting for transfers between devices, body(): lax.psum_scatter(sum_edge, 'edge', scatter_dimension=0, tiled=True)  76 us
    reduce_scatter x1, waiting for transfers between devices, body(): lax.psum_scatter(sum_send, 'edge', scatter_dimension=0, tiled=True)  73.1 us
    dot_general x63, matrix products, transposed_times(): lax.dot_general(left, right, (((0,), (0,)), ((), ())), preferred_element_...  70.9 us
  transfers between devices with their start and end apart: 31, of which 22 were waited for; matrix products, arithmetic and copies ran while one was open for 5% of the time, Pallas kernels for 0%

commit v1 on v0

--- a/solution.py
+++ b/solution.py
@@ -1,9 +1,26 @@
+import functools
 import jax
 import jax.numpy as jnp
 from jax import lax
 from jax.sharding import PartitionSpec as P
 
 BLOCK = 128
+
+
+def balance_plane(xx, which_axis):
+    count_all = lax.axis_size(which_axis)
+    item_now, x_new = (xx, 0)
+    while 1 << x_new < count_all:
+        panels = []
+        for k in range(count_all):
+            panels.append((k, k ^ 1 << x_new))
+        earlier = lax.ppermute(item_now, axis_name=which_axis, perm=panels)
+        item_now = item_now + earlier
+        x_new = x_new + 1
+    return item_now
+
+
+change_limits = functools.partial(balance_plane, which_axis="edge")
 
 
 def shifted(shard, axis, by):
@@ -125,7 +142,7 @@
         act = jax.nn.silu(pre).astype(jnp.bfloat16)
         message = matmul(act, weight_msg).astype(jnp.bfloat16)
         partial_agg = to_nodes(message, recv_blocks, recv_tiles)
-        aggregate = lax.psum(partial_agg, "edge")
+        aggregate = change_limits(partial_agg)
         agg_b = aggregate.astype(jnp.bfloat16)
         node_pre = matmul(feats, weight_node) + matmul(agg_b, weight_agg)
         node_act = jax.nn.silu(node_pre).astype(jnp.bfloat16)

time: 2040 us -> 1860 us (0.912)
  blocking collectives: 702 us -> 0 us
  waiting for transfers between devices: 946 us -> 1420 us
  starting transfers between devices: 23.3 us -> 82.8 us
  other arithmetic: 2.35 us -> 24 us
  local copies, waits for them, and re-layouts: 123 us -> 102 us
    psum x9 -> x0, blocking collectives: 702 us -> none  [advance(): aggregate = lax.psum(partial_agg, 'edge')]
    ppermute x0 -> x36, waiting for transfers between devices: none -> 430 us  [balance_plane(): earlier = lax.ppermute(item_now, axis_name=which_axis, perm=panels)]
    ppermute x0 -> x36, starting transfers between devices: none -> 59.5 us  [balance_plane(): earlier = lax.ppermute(item_now, axis_name=which_axis, perm=panels)]
    psum x9, waiting for transfers between devices: 630 us -> 669 us  [advance(): edge_terms = lax.psum(partial_back, 'edge')]
    while x558 -> x576, local copies, waits for them, and re-layouts: 96.3 us -> 74.5 us
  transfers between devices with their start and end apart: 31 -> 67, of which waited for: 22 -> 58; matrix products, arithmetic and copies ran while one was open for 5% -> 6% of each run, Pallas kernels for 0% -> 0%
where the time goes in v1:
time: 1860 us
  waiting for transfers between devices  1420 us (76%)
  matrix products  214 us (12%)
  local copies, waits for them, and re-layouts  102 us (5%)
  starting transfers between devices  82.8 us (4%)
  other arithmetic  24 us (1%)
    psum x9, waiting for transfers between devices, advance(): edge_terms = lax.psum(partial_back, 'edge')  669 us
    ppermute x36, waiting for transfers between devices, balance_plane(): earlier = lax.ppermute(item_now, axis_name=which_axis, perm=panels)  430 us
    reduce_scatter x1, waiting for transfers between devices, body(): lax.psum_scatter(sum_msg, 'edge', scatter_dimension=0, tiled=True)  76.5 us
    reduce_scatter x1, waiting for transfers between devices, body(): lax.psum_scatter(sum_recv, 'edge', scatter_dimension=0, tiled=True)  76.3 us
    reduce_scatter x1, waiting for transfers between devices, body(): lax.psum_scatter(sum_edge, 'edge', scatter_dimension=0, tiled=True)  76 us
    while x576, local copies, waits for them, and re-layouts  74.5 us
    reduce_scatter x1, waiting for transfers between devices, body(): lax.psum_scatter(sum_send, 'edge', scatter_dimension=0, tiled=True)  73.2 us
    dot_general x63, matrix products, transposed_times(): lax.dot_general(left, right, (((0,), (0,)), ((), ())), preferred_element_...  71.2 us
  transfers between devices with their start and end apart: 67, of which 58 were waited for; matrix products, arithmetic and copies ran while one was open for 6% of the time, Pallas kernels for 0%

profile of v1, /device:TPU:0, one launch (start us, length us, event | category | flops | bytes accessed | tf_op | source)
XLA Modules:
  0.0 1858.3 jit_solution(995033740483376372)
XLA Ops:
  14.2 1528.0 %while.36 = (s32[]{:T(128)}, bf16[256,512]{1,0:T(8,128)(2,1)}, bf16[256,512]{1,0:T(8,128)(2,1)}, f32[512,512]{1,0:T(8,128)}, f32[512,512]{1,0:T(8,128)}, /*index...) while((s32[]{:T(128)}, bf16[256,512]{1,0:T(8,128)(2,1)}, ...), condition=%wide.region_2.3_spmd.clone, body=%wide.region_0.2_spmd.clone.sunk | while | flops 2910724096 | bytes 153275056 | solution.py:203
  101.7 73.3 %all-reduce.2.cloned.1.call-done = f32[256,512]{1,0:T(8,128)} async-done(((f32[256,512]{1,0:T(8,128)}), f32[256,512]{1,0:T(8,128)}) %all-reduce.2.cloned.1.call-update) | async-done | bytes 524304 | tf_op jit(solution)/shard_map/while/body/eval_jaxpr/psum | solution.py:169
  215.6 12.6 collective-permute-done.2
  231.4 13.3 collective-permute-done.3
  270.8 74.4 %all-reduce.2.cloned.1.call-done = f32[256,512]{1,0:T(8,128)} async-done(((f32[256,512]{1,0:T(8,128)}), f32[256,512]{1,0:T(8,128)}) %all-reduce.2.cloned.1.call-update) | async-done | bytes 524304 | tf_op jit(solution)/shard_map/while/body/eval_jaxpr/psum | solution.py:169
  385.8 12.6 collective-permute-done.2
  401.5 13.2 collective-permute-done.3
  440.9 74.5 %all-reduce.2.cloned.1.call-done = f32[256,512]{1,0:T(8,128)} async-done(((f32[256,512]{1,0:T(8,128)}), f32[256,512]{1,0:T(8,128)}) %all-reduce.2.cloned.1.call-update) | async-done | bytes 524304 | tf_op jit(solution)/shard_map/while/body/eval_jaxpr/psum | solution.py:169
  571.7 13.2 collective-permute-done.3
  611.1 74.5 %all-reduce.2.cloned.1.call-done = f32[256,512]{1,0:T(8,128)} async-done(((f32[256,512]{1,0:T(8,128)}), f32[256,512]{1,0:T(8,128)}) %all-reduce.2.cloned.1.call-update) | async-done | bytes 524304 | tf_op jit(solution)/shard_map/while/body/eval_jaxpr/psum | solution.py:169
  742.0 13.2 collective-permute-done.3
  781.3 74.5 %all-reduce.2.cloned.1.call-done = f32[256,512]{1,0:T(8,128)} async-done(((f32[256,512]{1,0:T(8,128)}), f32[256,512]{1,0:T(8,128)}) %all-reduce.2.cloned.1.call-update) | async-done | bytes 524304 | tf_op jit(solution)/shard_map/while/body/eval_jaxpr/psum | solution.py:169
  912.2 13.2 collective-permute-done.3
  951.5 74.5 %all-reduce.2.cloned.1.call-done = f32[256,512]{1,0:T(8,128)} async-done(((f32[256,512]{1,0:T(8,128)}), f32[256,512]{1,0:T(8,128)}) %all-reduce.2.cloned.1.call-update) | async-done | bytes 524304 | tf_op jit(solution)/shard_map/while/body/eval_jaxpr/psum | solution.py:169
  1082.4 13.2 collective-permute-done.3
  1121.7 74.5 %all-reduce.2.cloned.1.call-done = f32[256,512]{1,0:T(8,128)} async-done(((f32[256,512]{1,0:T(8,128)}), f32[256,512]{1,0:T(8,128)}) %all-reduce.2.cloned.1.call-update) | async-done | bytes 524304 | tf_op jit(solution)/shard_map/while/body/eval_jaxpr/psum | solution.py:169
  1252.6 13.2 collective-permute-done.3
  1291.9 74.5 %all-reduce.2.cloned.1.call-done = f32[256,512]{1,0:T(8,128)} async-done(((f32[256,512]{1,0:T(8,128)}), f32[256,512]{1,0:T(8,128)}) %all-reduce.2.cloned.1.call-update) | async-done | bytes 524304 | tf_op jit(solution)/shard_map/while/body/eval_jaxpr/psum | solution.py:169
  1422.8 13.2 collective-permute-done.3
  1462.1 74.5 %all-reduce.2.cloned.1.call-done = f32[256,512]{1,0:T(8,128)} async-done(((f32[256,512]{1,0:T(8,128)}), f32[256,512]{1,0:T(8,128)}) %all-reduce.2.cloned.1.call-update) | async-done | bytes 524304 | tf_op jit(solution)/shard_map/while/body/eval_jaxpr/psum | solution.py:169
  1549.1 73.2 %reduce-scatter.5.cloned.1.call-done = f32[32,512]{1,0:T(8,128)} async-done(((f32[512,512]{1,0:T(8,128)}), f32[32,512]{1,0:T(8,128)}) %reduce-scatter.5.cloned.1.call-update) | async-done | bytes 65552 | tf_op jit(solution)/shard_map/reduce_scatter | solution.py:207
  1622.2 76.3 %reduce-scatter.7.cloned.1.call-done = f32[32,512]{1,0:T(8,128)} async-done(((f32[512,512]{1,0:T(8,128)}), f32[32,512]{1,0:T(8,128)}) %reduce-scatter.7.cloned.1.call-update) | async-done | bytes 65552 | tf_op jit(solution)/shard_map/reduce_scatter | solution.py:208
  1698.5 76.0 %reduce-scatter.9.cloned.1.call-done = f32[32,512]{1,0:T(8,128)} async-done(((f32[512,512]{1,0:T(8,128)}), f32[32,512]{1,0:T(8,128)}) %reduce-scatter.9.cloned.1.call-update) | async-done | bytes 65552 | tf_op jit(solution)/shard_map/reduce_scatter | solution.py:209
  1774.5 76.5 %reduce-scatter.11.cloned.1.call-done = f32[32,512]{1,0:T(8,128)} async-done(((f32[512,512]{1,0:T(8,128)}), f32[32,512]{1,0:T(8,128)}) %reduce-scatter.11.cloned.1.call-update) | async-done | bytes 65552 | tf_op jit(solution)/shard_map/reduce_scatter | solution.py:210
  (1116 shorter events, 736.1 us)
Async XLA Ops:
  14.2 160.8 %all-reduce.2.cloned.1.call-start = ((), (), s32[]{:S(2)}) async-start(), calls=%async_computation.8 | async-start | bytes 1048576 | tf_op jit(solution)/shard_map/while/body/eval_jaxpr/psum | solution.py:169
  97.5 81.1 %collective-permute-start.5 = (bf16[256,512]{1,0:T(8,128)(2,1)}, bf16[256,512]{1,0:T(8,128)(2,1)}, u32[]{:S(2)}, u32[]{:S(2)}) collective-permute-start(bf16[256,512]{1,0:T(8,128)(2,1)} %get-tuple-element.1012), channel_id=1, source_target_pairs={{16,0},{32,16},{48,32},{64,48},{80,64},{96,80},{112,96},{17,1},{33... | collective-permute-start | bytes 786440 | tf_op jit(solution)/shard_map/while/body/eval_jaxpr/ppermute | solution.py:29
  180.6 164.6 %all-reduce.2.cloned.1.call-start = ((), (), s32[]{:S(2)}) async-start(), calls=%async_computation.8 | async-start | bytes 1048576 | tf_op jit(solution)/shard_map/while/body/eval_jaxpr/psum | solution.py:169
  265.3 83.4 %collective-permute-start.5 = (bf16[256,512]{1,0:T(8,128)(2,1)}, bf16[256,512]{1,0:T(8,128)(2,1)}, u32[]{:S(2)}, u32[]{:S(2)}) collective-permute-start(bf16[256,512]{1,0:T(8,128)(2,1)} %get-tuple-element.1012), channel_id=1, source_target_pairs={{16,0},{32,16},{48,32},{64,48},{80,64},{96,80},{112,96},{17,1},{33... | collective-permute-start | bytes 786440 | tf_op jit(solution)/shard_map/while/body/eval_jaxpr/ppermute | solution.py:29
  350.7 164.6 %all-reduce.2.cloned.1.call-start = ((), (), s32[]{:S(2)}) async-start(), calls=%async_computation.8 | async-start | bytes 1048576 | tf_op jit(solution)/shard_map/while/body/eval_jaxpr/psum | solution.py:169
  398.5 16.3 collective-permute-start.3
  435.5 83.5 %collective-permute-start.5 = (bf16[256,512]{1,0:T(8,128)(2,1)}, bf16[256,512]{1,0:T(8,128)(2,1)}, u32[]{:S(2)}, u32[]{:S(2)}) collective-permute-start(bf16[256,512]{1,0:T(8,128)(2,1)} %get-tuple-element.1012), channel_id=1, source_target_pairs={{16,0},{32,16},{48,32},{64,48},{80,64},{96,80},{112,96},{17,1},{33... | collective-permute-start | bytes 786440 | tf_op jit(solution)/shard_map/while/body/eval_jaxpr/ppermute | solution.py:29
  520.9 164.6 %all-reduce.2.cloned.1.call-start = ((), (), s32[]{:S(2)}) async-start(), calls=%async_computation.8 | async-start | bytes 1048576 | tf_op jit(solution)/shard_map/while/body/eval_jaxpr/psum | solution.py:169
  568.7 16.3 collective-permute-start.3
  605.7 83.5 %collective-permute-start.5 = (bf16[256,512]{1,0:T(8,128)(2,1)}, bf16[256,512]{1,0:T(8,128)(2,1)}, u32[]{:S(2)}, u32[]{:S(2)}) collective-permute-start(bf16[256,512]{1,0:T(8,128)(2,1)} %get-tuple-element.1012), channel_id=1, source_target_pairs={{16,0},{32,16},{48,32},{64,48},{80,64},{96,80},{112,96},{17,1},{33... | collective-permute-start | bytes 786440 | tf_op jit(solution)/shard_map/while/body/eval_jaxpr/ppermute | solution.py:29
  691.2 164.6 %all-reduce.2.cloned.1.call-start = ((), (), s32[]{:S(2)}) async-start(), calls=%async_computation.8 | async-start | bytes 1048576 | tf_op jit(solution)/shard_map/while/body/eval_jaxpr/psum | solution.py:169
  775.9 83.5 %collective-permute-start.5 = (bf16[256,512]{1,0:T(8,128)(2,1)}, bf16[256,512]{1,0:T(8,128)(2,1)}, u32[]{:S(2)}, u32[]{:S(2)}) collective-permute-start(bf16[256,512]{1,0:T(8,128)(2,1)} %get-tuple-element.1012), channel_id=1, source_target_pairs={{16,0},{32,16},{48,32},{64,48},{80,64},{96,80},{112,96},{17,1},{33... | collective-permute-start | bytes 786440 | tf_op jit(solution)/shard_map/while/body/eval_jaxpr/ppermute | solution.py:29
  861.4 164.6 %all-reduce.2.cloned.1.call-start = ((), (), s32[]{:S(2)}) async-start(), calls=%async_computation.8 | async-start | bytes 1048576 | tf_op jit(solution)/shard_map/while/body/eval_jaxpr/psum | solution.py:169
  946.1 83.5 %collective-permute-start.5 = (bf16[256,512]{1,0:T(8,128)(2,1)}, bf16[256,512]{1,0:T(8,128)(2,1)}, u32[]{:S(2)}, u32[]{:S(2)}) collective-permute-start(bf16[256,512]{1,0:T(8,128)(2,1)} %get-tuple-element.1012), channel_id=1, source_target_pairs={{16,0},{32,16},{48,32},{64,48},{80,64},{96,80},{112,96},{17,1},{33... | collective-permute-start | bytes 786440 | tf_op jit(solution)/shard_map/while/body/eval_jaxpr/ppermute | solution.py:29
  1031.6 164.6 %all-reduce.2.cloned.1.call-start = ((), (), s32[]{:S(2)}) async-start(), calls=%async_computation.8 | async-start | bytes 1048576 | tf_op jit(solution)/shard_map/while/body/eval_jaxpr/psum | solution.py:169
  1116.3 83.5 %collective-permute-start.5 = (bf16[256,512]{1,0:T(8,128)(2,1)}, bf16[256,512]{1,0:T(8,128)(2,1)}, u32[]{:S(2)}, u32[]{:S(2)}) collective-permute-start(bf16[256,512]{1,0:T(8,128)(2,1)} %get-tuple-element.1012), channel_id=1, source_target_pairs={{16,0},{32,16},{48,32},{64,48},{80,64},{96,80},{112,96},{17,1},{33... | collective-permute-start | bytes 786440 | tf_op jit(solution)/shard_map/while/body/eval_jaxpr/ppermute | solution.py:29
  1201.8 164.6 %all-reduce.2.cloned.1.call-start = ((), (), s32[]{:S(2)}) async-start(), calls=%async_computation.8 | async-start | bytes 1048576 | tf_op jit(solution)/shard_map/while/body/eval_jaxpr/psum | solution.py:169
  1286.5 83.5 %collective-permute-start.5 = (bf16[256,512]{1,0:T(8,128)(2,1)}, bf16[256,512]{1,0:T(8,128)(2,1)}, u32[]{:S(2)}, u32[]{:S(2)}) collective-permute-start(bf16[256,512]{1,0:T(8,128)(2,1)} %get-tuple-element.1012), channel_id=1, source_target_pairs={{16,0},{32,16},{48,32},{64,48},{80,64},{96,80},{112,96},{17,1},{33... | collective-permute-start | bytes 786440 | tf_op jit(solution)/shard_map/while/body/eval_jaxpr/ppermute | solution.py:29
  1372.0 164.6 %all-reduce.2.cloned.1.call-start = ((), (), s32[]{:S(2)}) async-start(), calls=%async_computation.8 | async-start | bytes 1048576 | tf_op jit(solution)/shard_map/while/body/eval_jaxpr/psum | solution.py:169
  1456.7 83.5 %collective-permute-start.5 = (bf16[256,512]{1,0:T(8,128)(2,1)}, bf16[256,512]{1,0:T(8,128)(2,1)}, u32[]{:S(2)}, u32[]{:S(2)}) collective-permute-start(bf16[256,512]{1,0:T(8,128)(2,1)} %get-tuple-element.1012), channel_id=1, source_target_pairs={{16,0},{32,16},{48,32},{64,48},{80,64},{96,80},{112,96},{17,1},{33... | collective-permute-start | bytes 786440 | tf_op jit(solution)/shard_map/while/body/eval_jaxpr/ppermute | solution.py:29
  1542.2 80.1 %reduce-scatter.5.cloned.1.call-start = ((), (), s32[]{:S(2)}) async-start(), calls=%async_computation.4 | async-start | bytes 1114112 | tf_op jit(solution)/shard_map/reduce_scatter | solution.py:207
  1542.7 155.8 %reduce-scatter.7.cloned.1.call-start = ((), (), s32[]{:S(2)}) async-start(), calls=%async_computation.5 | async-start | bytes 1114112 | tf_op jit(solution)/shard_map/reduce_scatter | solution.py:208
  1543.3 231.2 %reduce-scatter.9.cloned.1.call-start = ((), (), s32[]{:S(2)}) async-start(), calls=%async_computation.6 | async-start | bytes 1114112 | tf_op jit(solution)/shard_map/reduce_scatter | solution.py:209
  1543.9 307.1 %reduce-scatter.11.cloned.1.call-start = ((), (), s32[]{:S(2)}) async-start(), calls=%async_computation.7 | async-start | bytes 1114112 | tf_op jit(solution)/shard_map/reduce_scatter | solution.py:210
  (336 other events, 2672.5 us)
Sparse Core Ops, SparseCore 0:
  89.3 85.6 all-reduce.1
  256.8 88.3 all-reduce.1
  426.9 88.4 all-reduce.1
  597.1 88.4 all-reduce.1
  767.3 88.4 all-reduce.1
  937.5 88.4 all-reduce.1
  1107.7 88.4 all-reduce.1
  1277.9 88.4 all-reduce.1
  1448.1 88.4 all-reduce.1
Sparse Core Ops, SparseCore 1:
  1546.4 75.8 reduce-scatter.4
  1626.2 72.3 reduce-scatter.6
  1702.2 72.3 reduce-scatter.8
  1778.6 72.3 reduce-scatter.10
